TPU v7x, 32 devices: a whole 2x2x4 slice. The times are simulated.
32 devices in a mesh: sec: 2 (over core), row: 4 (over y, x), col: 4 (over z).
Axes of the slice: x: 2, y: 2, z: 4, core: 2. Of those that a mesh axis runs over, the one named last changes fastest.
Arguments:
- anc_inverse: float32 [2048, 2048], P('row', ('sec', 'col')), as said below
- panel: float32 [8192, 2048], P(('sec', 'col'), 'row'), may hold values from -0.5 to 0.5
- diag_inverse: float32 [8192, 512], P(('sec', 'col')), may hold values from -6 to 6
- widths: int32 [16], replicated, may hold values from 1 to 4, as said below
- pattern: int32 [16, 16], replicated, may hold values 0 or 1
Outputs:
- off_inverse: float32 [8192, 2048], P(('sec', 'col'), 'row')
- child_inverse: float32 [8192, 512], P(('sec', 'col'))
Inputs may be any that keep to these rules, and one draw needn't show every extreme that they name: `anc_inverse`: exactly symmetric. `widths`: both 1 and 4 occur in every draw.
All inputs are finite; a program needn't handle non-finite values.
Results may differ from a plain program's by a relative error of at most 0.0003.
Values sent between devices are 32-bit elements; how exact they have to be, the bound alone decides.
A program may use at most 128 MiB of HBM per device.

v0:
```python
import jax
import jax.numpy as jnp
from jax import lax
from jax.sharding import PartitionSpec as P

B = 128
SW = 512


def mask_rows(values, slot_count, column_mask, block_mask, offset):
    amount = values.shape[1]
    window = lax.dynamic_slice_in_dim(block_mask, offset, amount, 1)
    shaped = (
        values.reshape(slot_count, SW, amount)
        * column_mask.reshape(slot_count, SW, 1)
        * window[:, None, :]
    )
    return shaped.reshape(slot_count * SW, amount)


def local(anc_inverse, panel, diag_inverse, widths, pattern):
    highest = lax.Precision.HIGHEST
    local_rows, rows_here = panel.shape
    slot_count = local_rows // SW
    slot_first = (lax.axis_index("sec") * lax.axis_size("col") + lax.axis_index("col")) * slot_count
    row_offset = lax.axis_index("row") * rows_here
    my_widths = lax.dynamic_slice_in_dim(widths, slot_first, slot_count)
    my_pattern = lax.dynamic_slice_in_dim(pattern, slot_first, slot_count, 0)
    block_mask = jnp.repeat(my_pattern.astype(jnp.float32), B, axis=1)
    position = jnp.arange(SW, dtype=jnp.int32)
    column_mask = (position[None, :] < my_widths[:, None] * B).astype(jnp.float32)
    anc_rows = lax.all_gather(anc_inverse, ("sec", "col"), axis=1, tiled=True)
    local_panel = mask_rows(panel, slot_count, column_mask, block_mask, row_offset)
    product = lax.psum_scatter(
        lax.dot_general(
            anc_rows,
            local_panel,
            (((0,), (1,)), ((), ())),
            precision=highest,
            preferred_element_type=jnp.float32,
        ),
        "row",
        scatter_dimension=0,
        tiled=True,
    ).T
    product = mask_rows(product, slot_count, column_mask, block_mask, row_offset)
    update = jnp.einsum(
        "jai,jbi->jab",
        product.reshape(slot_count, SW, rows_here),
        local_panel.reshape(slot_count, SW, rows_here),
        precision=highest,
    )
    summed = lax.psum(update.reshape(local_rows, SW), "row")
    pair_mask = column_mask[:, :, None] * column_mask[:, None, :]
    diag_block = (diag_inverse + summed) * pair_mask.reshape(local_rows, SW)
    return (-product, diag_block)


def solution(mesh):
    in_specs = (
        P("row", ("sec", "col")),
        P(("sec", "col"), "row"),
        P(("sec", "col"), None),
        P(),
        P(),
    )
    out_specs = (P(("sec", "col"), "row"), P(("sec", "col"), None))
    return jax.shard_map(local, mesh=mesh, in_specs=in_specs, out_specs=out_specs, check_vma=False)
```

profile of v0, /device:TPU:0, one launch (start us, length us, event | category | flops | bytes accessed | tf_op | source)
XLA Modules:
  0.0 249.4 jit_solution(4259381773065099106)
XLA Ops:
  7.2 0.0 all-gather.2.cloned.1.call-start
  7.2 0.7 all-gather.2.cloned.1.call-update
  7.9 0.0 reduce-scatter.2.cloned.1.call-start
  8.0 0.7 dynamic-slice_multiply_fusion
  8.7 0.1 compare_convert_fusion
  8.8 0.7 dynamic-slice_convert_fusion
  9.5 0.1 broadcast_bitcast_fusion
  9.6 1.8 bitcast_multiply_fusion.1
  11.4 47.8 %all-gather.2.cloned.1.call-done = f32[512,2048]{1,0:T(8,128)} async-done(((f32[512,256]{1,0:T(8,128)}), f32[512,2048]{1,0:T(8,128)}) %all-gather.2.cloned.1.call-update) | async-done | bytes 4194320 | tf_op jit(solution)/shard_map/all_gather | solution.py:32
  59.2 17.3 %convolution_bitcast_fusion = f32[2048,1024]{0,1:T(8,128)} fusion(f32[1024,512]{1,0:T(8,128)S(1)} %bitcast_multiply_fusion.1, f32[512,2048]{1,0:T(8,128)} %all-gather.2.cloned.1.call-done), kind=kOutput, calls=%fused_computation | convolution fusion | flops 12884901888 | bytes 14680064 | tf_op jit(solution)/shard_map/dot_general | solution.py:35
  76.5 0.0 copy-start
  76.5 0.0 reduce-scatter.2.cloned.1.call-update
  76.5 0.0 all-reduce.2.cloned.1.call-start
  76.6 85.2 %reduce-scatter.2.cloned.1.call-done = f32[512,1024]{0,1:T(8,128)} async-done(((f32[2048,1024]{0,1:T(8,128)}), f32[512,1024]{0,1:T(8,128)}) %reduce-scatter.2.cloned.1.call-update) | async-done | bytes 2097168 | tf_op jit(solution)/shard_map/reduce_scatter | solution.py:34
  161.8 0.0 copy-done
  161.8 6.7 %fusion.2 = f32[2,512,512]{2,1,0:T(8,128)} fusion(f32[2,512,512]{2,1,0:T(8,128)S(1)} %bitcast.29, f32[2,512,512]{2,1,0:T(8,128)} %bitcast.31, f32[2,512]{1,0:T(2,128)S(1)} %get-tuple-element.4, f32[2,512]{1,0:T(2,128)S(1)} %constant_dynamic-slice_fusion), kind=kOutput, calls=%fused_computation.7 | convolution fusion | flops 3223322624 | bytes 6299648 | tf_op jit(solution)/shard_map/jai,jbi->jab/dot_general | solution.py:47
  168.5 0.0 copy-start.1
  168.5 0.0 all-reduce.2.cloned.1.call-update
  168.6 69.7 %all-reduce.2.cloned.1.call-done = f32[1024,512]{1,0:T(8,128)} async-done(((f32[1024,512]{1,0:T(8,128)}), f32[1024,512]{1,0:T(8,128)}) %all-reduce.2.cloned.1.call-update) | async-done | bytes 2097168 | tf_op jit(solution)/shard_map/psum | solution.py:53
  238.2 0.0 copy-done.1
  238.2 4.7 %fusion.1 = (f32[1024,512]{1,0:T(8,128)}, f32[1024,512]{1,0:T(8,128)}) fusion(f32[1024,512]{1,0:T(8,128)} %param.7, f32[1024,512]{1,0:T(8,128)} %all-reduce.2.cloned.1.call-done, f32[2,512]{1,0:T(2,128)S(1)} %get-tuple-element.4, f32[1024]{0:T(1024)S(1)} %bitcast.33, f32[2,512]{1,0:T(2,128)S(1)} %constant_dynamic-slice_fusion, f32[512,1024]{0,1:T(8,128)S(1)} %copy-done.1), kind=kLoop, calls=%fused_computation.5 | loop fusion | flops 3145728 | bytes 10498048 | tf_op jit(solution)/shard_map/mul | solution.py:55
  (3 shorter events, 0.0 us)
Async XLA Ops:
  7.2 52.0 %all-gather.2.cloned.1.call-start = ((), (), s32[]{:S(2)}) async-start(), calls=%async_computation.1 | async-start | bytes 4718592 | tf_op jit(solution)/shard_map/all_gather | solution.py:32
  7.9 153.9 %reduce-scatter.2.cloned.1.call-start = ((), (), s32[]{:S(2)}) async-start(), calls=%async_computation.2 | async-start | bytes 10485760 | tf_op jit(solution)/shard_map/reduce_scatter | solution.py:34
  76.5 85.3 %copy-start = (f32[1024,512]{1,0:T(8,128)S(1)}, f32[1024,512]{1,0:T(8,128)}, u32[]{:S(2)}) copy-start(f32[1024,512]{1,0:T(8,128)} %param.6) | copy-start | bytes 6291460
  76.5 161.7 %all-reduce.2.cloned.1.call-start = ((), (), s32[]{:S(2)}) async-start(), calls=%async_computation.3 | async-start | bytes 4194304 | tf_op jit(solution)/shard_map/psum | solution.py:53
  168.5 69.7 %copy-start.1 = (f32[512,1024]{0,1:T(8,128)S(1)}, f32[512,1024]{0,1:T(8,128)}, u32[]{:S(2)}) copy-start(f32[512,1024]{0,1:T(8,128)} %reduce-scatter.2.cloned.1.call-done) | copy-start | bytes 6291460
Sparse Core Ops, SparseCore 0:
  9.6 49.5 all-gather.1
  76.6 85.1 reduce-scatter.1
  168.7 69.4 all-reduce.1
where the time goes:
time: 250 us; the launch traced here: 249 us
  waiting for transfers between devices  203 us (81%)
  matrix products  24 us (10%)
  between operations  13.8 us (6%)
  other arithmetic  8.03 us (3%)
    reduce_scatter x1, waiting for transfers between devices, local(): lax.psum_scatter(lax.dot_general(anc_rows, local_panel, (((0,), (1,)), ((...  85.2 us
    psum x1, waiting for transfers between devices, local(): summed = lax.psum(update.reshape(local_rows, SW), 'row')  69.7 us
    all_gather x1, waiting for transfers between devices, local(): anc_rows = lax.all_gather(anc_inverse, ('sec', 'col'), axis=1, tiled=True)  47.8 us
    dot_general x1, matrix products, local(): lax.dot_general(anc_rows, local_panel, (((0,), (1,)), ((), ())), precisio...  17.3 us
    dot_general x1, matrix products, local(): jnp.einsum('jai,jbi->jab', product.reshape(slot_count, SW, rows_here), lo...  6.73 us
  transfers between devices with their start and end apart: 3, of which 3 were waited for; matrix products, arithmetic and copies ran while one was open for 1% of the time, Pallas kernels for 0%

commit v1 on v0

--- a/solution.py
+++ b/solution.py
@@ -29,7 +29,10 @@
     block_mask = jnp.repeat(my_pattern.astype(jnp.float32), B, axis=1)
     position = jnp.arange(SW, dtype=jnp.int32)
     column_mask = (position[None, :] < my_widths[:, None] * B).astype(jnp.float32)
-    anc_rows = lax.all_gather(anc_inverse, ("sec", "col"), axis=1, tiled=True)
+    n_dev = lax.axis_size(("sec", "col"))
+    pieces = jnp.stack([anc_inverse for _ in range(n_dev)])
+    pieces = lax.all_to_all(pieces, ("sec", "col"), split_axis=0, concat_axis=0)
+    anc_rows = jnp.concatenate(pieces, axis=1)
     local_panel = mask_rows(panel, slot_count, column_mask, block_mask, row_offset)
     product = lax.psum_scatter(
         lax.dot_general(

time: 250 us -> 302 us (1.21)
  waiting for transfers between devices: 203 us -> 245 us
  starting transfers between devices: 0.12 us -> 6.74 us
  local copies, waits for them, and re-layouts: 0.11 us -> 3.83 us
    all_to_all x0 -> x1, waiting for transfers between devices: none -> 90.6 us  [local(): pieces = lax.all_to_all(pieces, ('sec', 'col'), split_axis=0, concat_axis=0)]
    all_gather x1 -> x0, waiting for transfers between devices: 47.8 us -> none  [local(): anc_rows = lax.all_gather(anc_inverse, ('sec', 'col'), axis=1, tiled=True)]
    all_to_all x0 -> x1, starting transfers between devices: none -> 6.49 us  [local(): pieces = lax.all_to_all(pieces, ('sec', 'col'), split_axis=0, concat_axis=0)]
where the time goes in v1:
time: 302 us; the launch traced here: 301 us
  waiting for transfers between devices  245 us (81%)
  matrix products  24.1 us (8%)
  between operations  14.1 us (5%)
  other arithmetic  7.38 us (2%)
  starting transfers between devices  6.74 us (2%)
  local copies, waits for them, and re-layouts  3.83 us (1%)
    all_to_all x1, waiting for transfers between devices, local(): pieces = lax.all_to_all(pieces, ('sec', 'col'), split_axis=0, concat_axis=0)  90.6 us
    reduce_scatter x1, waiting for transfers between devices, local(): lax.psum_scatter(lax.dot_general(anc_rows, local_panel, (((0,), (1,)), ((...  84.9 us
    psum x1, waiting for transfers between devices, local(): summed = lax.psum(update.reshape(local_rows, SW), 'row')  69.6 us
    dot_general x1, matrix products, local(): lax.dot_general(anc_rows, local_panel, (((0,), (1,)), ((), ())), precisio...  17.3 us
    dot_general x1, matrix products, local(): jnp.einsum('jai,jbi->jab', product.reshape(slot_count, SW, rows_here), lo...  6.73 us
    all_to_all x1, starting transfers between devices, local(): pieces = lax.all_to_all(pieces, ('sec', 'col'), split_axis=0, concat_axis=0)  6.49 us
  transfers between devices with their start and end apart: 3, of which 3 were waited for; matrix products, arithmetic and copies ran while one was open for 1% of the time, Pallas kernels for 0%

profile of v1, /device:TPU:0, one launch (start us, length us, event | category | flops | bytes accessed | tf_op | source)
XLA Modules:
  0.0 301.3 jit_solution(16830383895719228144)
XLA Ops:
  7.2 1.2 copy.7
  8.4 2.5 stack.2
  10.9 0.0 copy-start.2
  10.9 6.5 %all-to-all-start = ((f32[8,512,256]{1,2,0:T(8,128)}), f32[8,512,256]{1,2,0:T(8,128)}, u32[]{:S(2)}, u32[]{:S(2)}) async-start(f32[8,512,256]{1,2,0:T(8,128)} %stack.2), calls=%async_computation | async-start | bytes 8388608 | tf_op jit(solution)/shard_map/all_to_all | solution.py:34
  17.4 0.0 reduce-scatter.2.cloned.1.call-start
  17.4 0.0 copy-done.2
  17.4 0.1 dynamic-slice_multiply_fusion
  17.5 0.1 compare_convert_fusion
  17.6 0.7 dynamic-slice_convert_fusion
  18.3 0.1 broadcast_bitcast_fusion
  18.4 1.8 bitcast_multiply_fusion.1
  20.2 90.6 %all-to-all-done = f32[8,512,256]{1,2,0:T(8,128)} async-done(((f32[8,512,256]{1,2,0:T(8,128)}), f32[8,512,256]{1,2,0:T(8,128)}, u32[]{:S(2)}, u32[]{:S(2)}) %all-to-all-start) | async-done | bytes 4194336 | tf_op jit(solution)/shard_map/all_to_all | solution.py:34
  110.9 17.3 %convolution_bitcast_fusion = f32[2048,1024]{0,1:T(8,128)} fusion(f32[1024,512]{1,0:T(8,128)S(1)} %bitcast_multiply_fusion.1, f32[512,2048]{0,1:T(8,128)} %bitcast.2), kind=kOutput, calls=%fused_computation | convolution fusion | flops 12884901888 | bytes 14680064 | tf_op jit(solution)/shard_map/dot_general | solution.py:38
  128.2 0.0 copy-start
  128.2 0.0 reduce-scatter.2.cloned.1.call-update
  128.2 0.2 all-reduce.2.cloned.1.call-start
  128.5 84.9 %reduce-scatter.2.cloned.1.call-done = f32[512,1024]{0,1:T(8,128)} async-done(((f32[2048,1024]{0,1:T(8,128)}), f32[512,1024]{0,1:T(8,128)}) %reduce-scatter.2.cloned.1.call-update) | async-done | bytes 2097168 | tf_op jit(solution)/shard_map/reduce_scatter | solution.py:37
  213.4 0.0 copy-done
  213.4 6.7 %fusion.2 = f32[2,512,512]{2,1,0:T(8,128)} fusion(f32[2,512,512]{2,1,0:T(8,128)S(1)} %bitcast.32, f32[2,512,512]{2,1,0:T(8,128)} %bitcast.34, f32[2,512]{1,0:T(2,128)S(1)} %get-tuple-element.4, f32[2,512]{1,0:T(2,128)S(1)} %constant_dynamic-slice_fusion), kind=kOutput, calls=%fused_computation.7 | convolution fusion | flops 3223322624 | bytes 6299648 | tf_op jit(solution)/shard_map/jai,jbi->jab/dot_general | solution.py:50
  220.1 0.0 copy-start.1
  220.1 0.0 all-reduce.2.cloned.1.call-update
  220.1 69.6 %all-reduce.2.cloned.1.call-done = f32[1024,512]{1,0:T(8,128)} async-done(((f32[1024,512]{1,0:T(8,128)}), f32[1024,512]{1,0:T(8,128)}) %all-reduce.2.cloned.1.call-update) | async-done | bytes 2097168 | tf_op jit(solution)/shard_map/psum | solution.py:56
  289.7 0.0 copy-done.1
  289.7 4.7 %fusion.1 = (f32[1024,512]{1,0:T(8,128)}, f32[1024,512]{1,0:T(8,128)}) fusion(f32[1024,512]{1,0:T(8,128)} %param.7, f32[1024,512]{1,0:T(8,128)} %all-reduce.2.cloned.1.call-done, f32[2,512]{1,0:T(2,128)S(1)} %get-tuple-element.4, f32[1024]{0:T(1024)S(1)} %bitcast.36, f32[2,512]{1,0:T(2,128)S(1)} %constant_dynamic-slice_fusion, f32[512,1024]{0,1:T(8,128)S(1)} %copy-done.1), kind=kLoop, calls=%fused_computation.5 | loop fusion | flops 3145728 | bytes 10498048 | tf_op jit(solution)/shard_map/mul | solution.py:58
  (3 shorter events, 0.0 us)
Async XLA Ops:
  10.9 6.5 %copy-start.2 = (s32[16]{0:T(128)S(1)}, s32[16]{0:T(128)}, u32[]{:S(2)}) copy-start(s32[16]{0:T(128)} %param.8) | copy-start | bytes 196
  10.9 100.0 %all-to-all-start = ((f32[8,512,256]{1,2,0:T(8,128)}), f32[8,512,256]{1,2,0:T(8,128)}, u32[]{:S(2)}, u32[]{:S(2)}) async-start(f32[8,512,256]{1,2,0:T(8,128)} %stack.2), calls=%async_computation | async-start | bytes 8388608 | tf_op jit(solution)/shard_map/all_to_all | solution.py:34
  17.4 196.0 %reduce-scatter.2.cloned.1.call-start = ((), (), s32[]{:S(2)}) async-start(), calls=%async_computation.2 | async-start | bytes 10485760 | tf_op jit(solution)/shard_map/reduce_scatter | solution.py:37
  128.2 85.2 %copy-start = (f32[1024,512]{1,0:T(8,128)S(1)}, f32[1024,512]{1,0:T(8,128)}, u32[]{:S(2)}) copy-start(f32[1024,512]{1,0:T(8,128)} %param.6) | copy-start | bytes 6291460
  128.2 161.5 %all-reduce.2.cloned.1.call-start = ((), (), s32[]{:S(2)}) async-start(), calls=%async_computation.3 | async-start | bytes 4194304 | tf_op jit(solution)/shard_map/psum | solution.py:56
  220.1 69.6 %copy-start.1 = (f32[512,1024]{0,1:T(8,128)S(1)}, f32[512,1024]{0,1:T(8,128)}, u32[]{:S(2)}) copy-start(f32[512,1024]{0,1:T(8,128)} %reduce-scatter.2.cloned.1.call-done) | copy-start | bytes 6291460
Sparse Core Ops, SparseCore 0:
  128.4 84.9 reduce-scatter.1
  220.2 69.4 all-reduce.1

commit v2 on v0

--- a/solution.py
+++ b/solution.py
@@ -50,7 +50,9 @@
         local_panel.reshape(slot_count, SW, rows_here),
         precision=highest,
     )
-    summed = lax.psum(update.reshape(local_rows, SW), "row")
+    own = update.reshape(local_rows, SW)
+    parts = lax.all_gather(own, "row")
+    summed = jnp.sum(parts, axis=0)
     pair_mask = column_mask[:, :, None] * column_mask[:, None, :]
     diag_block = (diag_inverse + summed) * pair_mask.reshape(local_rows, SW)
     return (-product, diag_block)

time: 250 us -> 274 us (1.096)
  waiting for transfers between devices: 203 us -> 221 us
  other arithmetic: 8.03 us -> 14 us
    all_gather x0 -> x1, waiting for transfers between devices: none -> 87.6 us  [local(): parts = lax.all_gather(own, 'row')]
    psum x1 -> x0, waiting for transfers between devices: 69.7 us -> none  [local(): summed = lax.psum(update.reshape(local_rows, SW), 'row')]
    reduce_sum x0 -> x1, other arithmetic: none -> 5.95 us  [local(): summed = jnp.sum(parts, axis=0)]
where the time goes in v2:
time: 274 us; the launch traced here: 273 us
  waiting for transfers between devices  221 us (81%)
  matrix products  24 us (9%)
  other arithmetic  14 us (5%)
  between operations  13.8 us (5%)
    all_gather x1, waiting for transfers between devices, local(): parts = lax.all_gather(own, 'row')  87.6 us
    reduce_scatter x1, waiting for transfers between devices, local(): lax.psum_scatter(lax.dot_general(anc_rows, local_panel, (((0,), (1,)), ((...  85 us
    all_gather x1, waiting for transfers between devices, local(): anc_rows = lax.all_gather(anc_inverse, ('sec', 'col'), axis=1, tiled=True)  47.8 us
    dot_general x1, matrix products, local(): lax.dot_general(anc_rows, local_panel, (((0,), (1,)), ((), ())), precisio...  17.3 us
    dot_general x1, matrix products, local(): jnp.einsum('jai,jbi->jab', product.reshape(slot_count, SW, rows_here), lo...  6.73 us
    reduce_sum x1, other arithmetic, local(): summed = jnp.sum(parts, axis=0)  5.95 us
  transfers between devices with their start and end apart: 3, of which 3 were waited for; matrix products, arithmetic and copies ran while one was open for 1% of the time, Pallas kernels for 0%

profile of v2, /device:TPU:0, one launch (start us, length us, event | category | flops | bytes accessed | tf_op | source)
XLA Modules:
  0.0 273.4 jit_solution(8294116059753729394)
XLA Ops:
  7.2 0.0 all-gather.3.cloned.1.call-start
  7.2 0.7 all-gather.3.cloned.1.call-update
  7.9 0.0 reduce-scatter.2.cloned.1.call-start
  8.0 0.7 dynamic-slice_multiply_fusion
  8.7 0.1 compare_convert_fusion
  8.8 0.7 dynamic-slice_convert_fusion
  9.5 0.1 broadcast_bitcast_fusion
  9.6 1.8 bitcast_multiply_fusion.1
  11.4 47.8 %all-gather.3.cloned.1.call-done = f32[512,2048]{1,0:T(8,128)} async-done(((f32[512,256]{1,0:T(8,128)}), f32[512,2048]{1,0:T(8,128)}) %all-gather.3.cloned.1.call-update) | async-done | bytes 4194320 | tf_op jit(solution)/shard_map/all_gather | solution.py:32
  59.2 17.3 %convolution_bitcast_fusion = f32[2048,1024]{0,1:T(8,128)} fusion(f32[1024,512]{1,0:T(8,128)S(1)} %bitcast_multiply_fusion.1, f32[512,2048]{1,0:T(8,128)} %all-gather.3.cloned.1.call-done), kind=kOutput, calls=%fused_computation | convolution fusion | flops 12884901888 | bytes 14680064 | tf_op jit(solution)/shard_map/dot_general | solution.py:35
  76.5 0.0 copy-start
  76.5 0.0 reduce-scatter.2.cloned.1.call-update
  76.5 0.2 all-gather.5.cloned.1.call-start
  76.8 85.0 %reduce-scatter.2.cloned.1.call-done = f32[512,1024]{0,1:T(8,128)} async-done(((f32[2048,1024]{0,1:T(8,128)}), f32[512,1024]{0,1:T(8,128)}) %reduce-scatter.2.cloned.1.call-update) | async-done | bytes 2097168 | tf_op jit(solution)/shard_map/reduce_scatter | solution.py:34
  161.8 0.0 copy-done
  161.8 6.7 %fusion.2 = f32[2,512,512]{2,1,0:T(8,128)} fusion(f32[2,512,512]{2,1,0:T(8,128)S(1)} %bitcast.29, f32[2,512,512]{2,1,0:T(8,128)} %bitcast.31, f32[2,512]{1,0:T(2,128)S(1)} %get-tuple-element.4, f32[2,512]{1,0:T(2,128)S(1)} %constant_dynamic-slice_fusion), kind=kOutput, calls=%fused_computation.7 | convolution fusion | flops 3223322624 | bytes 6299648 | tf_op jit(solution)/shard_map/jai,jbi->jab/dot_general | solution.py:47
  168.5 0.0 all-gather.5.cloned.1.call-update
  168.6 0.0 copy-start.1
  168.6 87.6 %all-gather.5.cloned.1.call-done = f32[4,1024,512]{2,1,0:T(8,128)} async-done(((f32[1,1024,512]{2,1,0:T(8,128)}), f32[4,1024,512]{2,1,0:T(8,128)}) %all-gather.5.cloned.1.call-update) | async-done | bytes 8388624 | tf_op jit(solution)/shard_map/all_gather | solution.py:54
  256.2 6.0 %reduce_sum.9 = f32[1024,512]{1,0:T(8,128)} reduce(f32[4,1024,512]{2,1,0:T(8,128)} %all-gather.5.cloned.1.call-done, f32[]{:T(128)} %constant.28.clone.1), dimensions={0}, to_apply=%region_1.0 | reduce | flops 1572864 | bytes 10485764 | tf_op jit(solution)/shard_map/reduce_sum | solution.py:55
  262.2 0.0 copy-done.1
  262.2 4.7 %fusion.1 = (f32[1024,512]{1,0:T(8,128)}, f32[1024,512]{1,0:T(8,128)}) fusion(f32[1024,512]{1,0:T(8,128)} %param.7, f32[1024,512]{1,0:T(8,128)} %reduce_sum.9, f32[2,512]{1,0:T(2,128)S(1)} %get-tuple-element.4, f32[1024]{0:T(1024)S(1)} %bitcast.33, f32[2,512]{1,0:T(2,128)S(1)} %constant_dynamic-slice_fusion, f32[512,1024]{0,1:T(8,128)S(1)} %copy-done.1), kind=kLoop, calls=%fused_computation.5 | loop fusion | flops 3145728 | bytes 10498048 | tf_op jit(solution)/shard_map/mul | solution.py:57
  (3 shorter events, 0.0 us)
Async XLA Ops:
  7.2 52.0 %all-gather.3.cloned.1.call-start = ((), (), s32[]{:S(2)}) async-start(), calls=%async_computation.1 | async-start | bytes 4718592 | tf_op jit(solution)/shard_map/all_gather | solution.py:32
  7.9 153.9 %reduce-scatter.2.cloned.1.call-start = ((), (), s32[]{:S(2)}) async-start(), calls=%async_computation.2 | async-start | bytes 10485760 | tf_op jit(solution)/shard_map/reduce_scatter | solution.py:34
  76.5 85.3 %copy-start = (f32[1024,512]{1,0:T(8,128)S(1)}, f32[1024,512]{1,0:T(8,128)}, u32[]{:S(2)}) copy-start(f32[1024,512]{1,0:T(8,128)} %param.6) | copy-start | bytes 6291460
  76.5 179.7 %all-gather.5.cloned.1.call-start = ((), (), s32[]{:S(2)}) async-start(), calls=%async_computation.3 | async-start | bytes 10485760 | tf_op jit(solution)/shard_map/all_gather | solution.py:54
  168.6 93.6 %copy-start.1 = (f32[512,1024]{0,1:T(8,128)S(1)}, f32[512,1024]{0,1:T(8,128)}, u32[]{:S(2)}) copy-start(f32[512,1024]{0,1:T(8,128)} %reduce-scatter.2.cloned.1.call-done) | copy-start | bytes 6291460
Sparse Core Ops, SparseCore 0:
  9.6 49.5 all-gather.2
  76.6 85.1 reduce-scatter.1
  168.7 87.4 all-gather.4
